TPU v7x, 32 devices: a whole 2x2x4 slice. The times are simulated.
32 devices in a mesh: dp: 4 (over y, core), head: 8 (over z, x).
Axes of the slice: x: 2, y: 2, z: 4, core: 2. Of those that a mesh axis runs over, the one named last changes fastest.
Arguments:
- hidden: bfloat16 [12288, 4096], P('dp'), may hold values from -6 to 6
- weight: bfloat16 [2048, 4096], P('head'), may hold values from -0.09375 to 0.09375
- block_ids: int32 [48, 8], P('dp'), may hold values from 0 to 15, all different within a row
- targets: int32 [12288, 8], P('dp'), may hold values from 0 to 2047
Outputs:
- grad_hidden: bfloat16 [12288, 4096], P('dp', 'head')
- grad_weight: bfloat16 [2048, 4096], P('head', 'dp')
Inputs may be any that keep to these rules, and one draw needn't show every extreme that they name: `block_ids`: each row block lists 8 different label blocks; every label block is listed by some row block. `targets`: a row may repeat a label id.
All inputs are finite; a program needn't handle non-finite values.
Results may differ from a plain program's by a relative error of at most 0.014.
Values may be sent and summed in bfloat16 or wider, within the bound.
No kernel may reach another device: no remote copies, remote signals or barrier semaphores. Data moves between devices by JAX's collectives and lax.ppermute only.
A program may use at most 192 MiB of HBM per device.

v0:
```python
import jax
import jax.numpy as jnp
from jax import lax
from jax.sharding import PartitionSpec as P

BLOCK = 128


def local(hidden, weight, block_ids, targets):
    head_count = lax.axis_size("head")
    device = lax.axis_index("head")
    owned = weight.shape[0]
    per_device = owned // BLOCK
    row_blocks = block_ids.shape[0]
    block_rows = hidden.shape[0] // row_blocks
    first = device * per_device
    owned_ids = first + jnp.arange(per_device, dtype=jnp.int32)
    logits = jnp.einsum("rd,ld->rl", hidden, weight, preferred_element_type=jnp.float32)
    slot_match = block_ids[:, :, None] == owned_ids[None, None, :]
    listed = jnp.any(slot_match, axis=1)
    row_mask = jnp.broadcast_to(
        listed[:, None, :, None], (row_blocks, block_rows, per_device, BLOCK)
    )
    row_mask = row_mask.reshape(row_blocks * block_rows, owned)
    labels = first * BLOCK + jnp.arange(owned, dtype=jnp.int32)
    hits = jnp.any(targets[:, :, None] == labels[None, None, :], axis=1)
    signal = jax.nn.sigmoid(logits) - hits.astype(jnp.float32)
    grads = jnp.where(row_mask, signal, 0.0).astype(jnp.bfloat16)
    weight_part = jnp.einsum("rl,rd->ld", grads, hidden, preferred_element_type=jnp.float32)
    grad_weight = lax.psum_scatter(
        weight_part.astype(jnp.bfloat16), "dp", scatter_dimension=1, tiled=True
    )
    grads4 = grads.reshape(row_blocks, block_rows, per_device, BLOCK)
    picker = slot_match.astype(jnp.bfloat16)
    slot_local = jnp.einsum(
        "ikb,irbj->ikrj", picker, grads4, preferred_element_type=jnp.float32
    ).astype(jnp.bfloat16)
    slot_total = lax.psum(slot_local, "head").astype(jnp.float32).astype(jnp.bfloat16)
    columns = lax.all_to_all(weight, "head", split_axis=1, concat_axis=0, tiled=True)
    narrow = columns.shape[1]
    blocks3 = columns.reshape(per_device * head_count, BLOCK, narrow)
    chosen = blocks3[block_ids]
    terms = jnp.einsum("ikrj,ikjd->ikrd", slot_total, chosen, preferred_element_type=jnp.float32)
    groups = jnp.arange(head_count, dtype=jnp.int32)
    owner = ((block_ids // per_device)[:, :, None] == groups[None, None, :]).astype(jnp.float32)
    parts = jnp.einsum("iko,ikrd->iord", owner, terms, precision=lax.Precision.HIGHEST)
    rounded = lax.optimization_barrier(parts.astype(jnp.bfloat16))
    summed = jnp.sum(rounded.astype(jnp.float32), axis=1)
    grad_hidden = summed.reshape(row_blocks * block_rows, narrow).astype(jnp.bfloat16)
    return (grad_hidden, grad_weight)


def solution(mesh):
    return jax.shard_map(
        local,
        mesh=mesh,
        in_specs=(P("dp", None), P("head", None), P("dp", None), P("dp", None)),
        out_specs=(P("dp", "head"), P("head", "dp")),
        check_vma=False,
    )
```

profile of v0, /device:TPU:0, one launch (start us, length us, event | category | flops | bytes accessed | tf_op | source)
XLA Modules:
  0.0 421.9 jit_solution(15903401731539270005)
XLA Ops:
  8.0 0.0 all-reduce.2.cloned.1.call-start
  8.1 0.8 copy.35
  8.8 0.4 compare_reduce_fusion.1
  9.2 0.1 copy.36
  9.3 0.3 broadcast_in_dim.7
  9.7 0.5 copy.46
  10.2 1.8 copy.38
  12.0 1.4 copy.37
  13.3 17.2 %compare_reduce_fusion = pred[3072,256]{1,0:T(8,128)(4,1)S(1)} fusion(s32[256]{0:T(256)S(1)} %iota_add_fusion, s32[3072,8]{1,0:T(8,128)S(1)} %copy.37), kind=kLoop, calls=%fused_computation.3 | loop fusion | flops 11796480 | bytes 885760 | tf_op jit(solution)/shard_map/reduce_or | solution.py:26
  30.5 13.2 %fusion.12 = bf16[3072,256]{1,0:T(8,128)(2,1)S(1)} fusion(pred[3072,256]{1,0:T(32,128)(4,1)} %copy.38, bf16[3072,4096]{1,0:T(8,128)(2,1)} %param.4, bf16[256,4096]{1,0:T(8,128)(2,1)} %param.5, pred[3072,256]{1,0:T(8,128)(4,1)S(1)} %compare_reduce_fusion), kind=kOutput, calls=%fused_computation.14 | convolution fusion | flops 6447955968 | bytes 30408704 | tf_op jit(solution)/shard_map/rd,ld->rl/dot_general | solution.py:18
  43.7 0.0 copy-start.1
  43.7 0.4 reshape.32
  44.2 4.5 %convolution_convert_fusion.1 = bf16[12,8,256,128]{3,1,2,0:T(8,128)(2,1)} fusion(bf16[12,256,2,128]{3,2,1,0:T(2,128)(2,1)S(1)} %reshape.32, s32[12,8]{1,0:T(8,128)S(1)} %copy.35, s32[2]{0:T(128)S(1)} %iota_add_fusion.1), kind=kOutput, calls=%fused_computation.15 | convolution fusion | flops 15728832 | bytes 7864712 | tf_op jit(solution)/shard_map/ikb,irbj->ikrj/dot_general | solution.py:35
  48.7 0.0 all-reduce.2.cloned.1.call-update
  48.7 0.0 copy-done.1
  48.7 4.1 copy.39
  52.8 7.3 %all-to-all-start = ((bf16[256,8,512]{0,2,1:T(8,128)(2,1)}), bf16[256,8,512]{0,2,1:T(8,128)(2,1)S(1)}, u32[]{:S(2)}, u32[]{:S(2)}) async-start(bf16[256,8,512]{0,2,1:T(8,128)(2,1)} %bitcast.29), calls=%async_computation | async-start | bytes 4194304 | tf_op jit(solution)/shard_map/all_to_all | solution.py:39
  60.1 0.0 copy-start.2
  60.1 0.2 reduce-scatter.2.cloned.1.call-start
  60.3 13.1 %convolution_convert_fusion = bf16[256,4096]{1,0:T(8,128)(2,1)} fusion(bf16[3072,256]{1,0:T(8,128)(2,1)} %copy-done.1, bf16[3072,4096]{1,0:T(8,128)(2,1)} %param.4), kind=kOutput, calls=%fused_computation.7 | convolution fusion | flops 6443499520 | bytes 28835840 | tf_op jit(solution)/shard_map/rl,rd->ld/dot_general | solution.py:29
  73.5 0.0 reduce-scatter.2.cloned.1.call-update
  73.5 0.0 copy-done.2
  73.5 0.1 copy.34
  73.6 0.1 copy.41
  73.7 0.1 reshape.36
  73.8 84.4 %all-to-all-done = bf16[256,8,512]{0,2,1:T(8,128)(2,1)S(1)} async-done(((bf16[256,8,512]{0,2,1:T(8,128)(2,1)}), bf16[256,8,512]{0,2,1:T(8,128)(2,1)S(1)}, u32[]{:S(2)}, u32[]{:S(2)}) %all-to-all-start) | async-done | bytes 2097184 | tf_op jit(solution)/shard_map/all_to_all | solution.py:39
  158.1 0.0 copy-start
  158.1 1.3 copy-done
  159.5 2.9 copy.40
  162.3 6.7 %gather_fusion = bf16[96,128,512]{2,1,0:T(8,128)(2,1)} fusion(bf16[16,128,512]{2,1,0:T(8,128)(2,1)S(1)} %bitcast.26, s32[1024]{0:T(1024)S(1)} %pad_clamp_fusion), kind=kCustom, calls=%fused_computation | custom fusion | bytes 25166208 | tf_op jit(solution)/shard_map/gather | solution.py:42
  169.1 137.8 %all-reduce.2.cloned.1.call-done = bf16[12,8,256,128]{3,1,2,0:T(8,128)(2,1)} async-done(((bf16[12,8,256,128]{3,1,2,0:T(8,128)(2,1)}), bf16[12,8,256,128]{3,1,2,0:T(8,128)(2,1)}) %all-reduce.2.cloned.1.call-update) | async-done | bytes 6291472 | tf_op jit(solution)/shard_map/psum | solution.py:38
  306.9 24.0 %fusion.5 = f32[12,8,256,512]{3,2,1,0:T(8,128)} fusion(bf16[12,8,128,512]{3,2,1,0:T(8,128)(2,1)} %bitcast.27, bf16[12,8,256,128]{3,1,2,0:T(8,128)(2,1)} %all-reduce.2.cloned.1.call-done), kind=kOutput, calls=%fused_computation.5 | convolution fusion | flops 3221225472 | bytes 69206016 | tf_op jit(solution)/shard_map/ikrj,ikjd->ikrd/dot_general | solution.py:43
  330.9 61.9 %fusion.2 = bf16[12,8,256,512]{3,1,2,0:T(8,128)(2,1)} fusion(f32[12,8,256,512]{3,2,1,0:T(8,128)} %fusion.5, s32[12,8]{1,0:T(8,128)S(1)} %copy.34), kind=kOutput, calls=%fused_computation.4 | convolution fusion | flops 1220543232 | bytes 75497856 | tf_op jit(solution)/shard_map/iko,ikrd->iord/dot_general | solution.py:46
  392.8 21.7 %reduce_sum.12 = bf16[12,256,512]{2,1,0:T(8,128)(2,1)} reduce(bf16[12,8,256,512]{3,1,2,0:T(8,128)(2,1)} %fusion.2, bf16[]{:T(256)} %constant.32.clone.1), dimensions={1}, to_apply=%region_3.4 | reduce | flops 11010048 | bytes 28311554 | tf_op jit(solution)/shard_map/reduce_sum | solution.py:48
  414.5 0.0 reduce-scatter.2.cloned.1.call-done
  (4 shorter events, 0.0 us)
Async XLA Ops:
  8.0 298.9 %all-reduce.2.cloned.1.call-start = ((), (), s32[]{:S(2)}) async-start(), calls=%async_computation.2 | async-start | bytes 12582912 | tf_op jit(solution)/shard_map/psum | solution.py:38
  43.7 5.0 %copy-start.1 = (bf16[3072,256]{1,0:T(8,128)(2,1)}, bf16[3072,256]{1,0:T(8,128)(2,1)S(1)}, u32[]{:S(2)}) copy-start(bf16[3072,256]{1,0:T(8,128)(2,1)S(1)} %fusion.12) | copy-start | bytes 4718596
  52.8 105.3 %all-to-all-start = ((bf16[256,8,512]{0,2,1:T(8,128)(2,1)}), bf16[256,8,512]{0,2,1:T(8,128)(2,1)S(1)}, u32[]{:S(2)}, u32[]{:S(2)}) async-start(bf16[256,8,512]{0,2,1:T(8,128)(2,1)} %bitcast.29), calls=%async_computation | async-start | bytes 4194304 | tf_op jit(solution)/shard_map/all_to_all | solution.py:39
  60.1 13.4 %copy-start.2 = (s32[12,8]{0,1:T(8,128)S(1)}, s32[12,8]{0,1:T(8,128)}, u32[]{:S(2)}) copy-start(s32[12,8]{0,1:T(8,128)} %param.6) | copy-start | bytes 1156
  60.1 354.4 %reduce-scatter.2.cloned.1.call-start = ((), (), s32[]{:S(2)}) async-start(), calls=%async_computation.3 | async-start | bytes 2621440 | tf_op jit(solution)/shard_map/reduce_scatter | solution.py:30
  158.1 1.3 copy-start
Sparse Core Ops, SparseCore 0:
  48.9 257.9 all-reduce.1
Sparse Core Ops, SparseCore 1:
  73.6 32.3 reduce-scatter.1
where the time goes:
time: 423 us; the launch traced here: 422 us
  waiting for transfers between devices  222 us (52%)
  matrix products  117 us (28%)
  other arithmetic  39.2 us (9%)
  local copies, waits for them, and re-layouts  20.6 us (5%)
  between operations  15.6 us (4%)
  starting transfers between devices  7.54 us (2%)
    psum x1, waiting for transfers between devices, local(): lax.psum(slot_local, 'head').astype(jnp.float32).astype(jnp.bfloat16)  138 us
    all_to_all x1, waiting for transfers between devices, local(): lax.all_to_all(weight, 'head', split_axis=1, concat_axis=0, tiled=True)  84.4 us
    dot_general x1, matrix products, local(): jnp.einsum('iko,ikrd->iord', owner, terms, precision=lax.Precision.HIGHEST)  61.9 us
    dot_general x1, matrix products, local(): jnp.einsum('ikrj,ikjd->ikrd', slot_total, chosen, preferred_element_type=...  24 us
    reduce_sum x1, other arithmetic, local(): summed = jnp.sum(rounded.astype(jnp.float32), axis=1)  21.7 us
    reduce_or x1, other arithmetic, local(): hits = jnp.any(targets[:, :, None] == labels[None, None, :], axis=1)  17.2 us
    dot_general x1, matrix products, local(): jnp.einsum('rd,ld->rl', hidden, weight, preferred_element_type=jnp.float32)  13.2 us
    dot_general x1, matrix products, local(): jnp.einsum('rl,rd->ld', grads, hidden, preferred_element_type=jnp.float32)  13.1 us
  transfers between devices with their start and end apart: 3, of which 2 were waited for; matrix products, arithmetic and copies ran while one was open for 32% of the time, Pallas kernels for 0%

commit v1 on v0

v1 whole, which is shorter than its diff:
```python
import functools

import jax
import jax.numpy as jnp
import numpy as np
from jax import lax
from jax.experimental import pallas as pl
from jax.experimental.pallas import tpu as pltpu
from jax.sharding import PartitionSpec as P


BLOCK = 128
PAIR = 2 * BLOCK
Z = 4


def ring_order(heads):
    order = []
    for x in range(heads // Z):
        zs = range(Z) if x % 2 == 0 else reversed(range(Z))
        order += [z * (heads // Z) + x for z in zs]
    return order


def signal_of(logits, targets, labels):
    hit = targets[:, 0:1] == labels
    for p in range(1, targets.shape[1]):
        hit = jnp.logical_or(hit, targets[:, p : p + 1] == labels)
    prob = 0.5 * jnp.tanh(0.5 * logits) + 0.5
    return prob - hit.astype(jnp.float32)


def listed_flag(ids_ref, i, block):
    flag = ids_ref[0, i] == block
    for k in range(1, ids_ref.shape[0]):
        flag = jnp.logical_or(flag, ids_ref[k, i] == block)
    return flag.astype(jnp.int32)


def lanes():
    return lax.broadcasted_iota(jnp.int32, (1, PAIR), 1)


def nt(a, b):
    return lax.dot_general(a, b, (((1,), (1,)), ((), ())), preferred_element_type=jnp.float32)


def tn(a, b):
    return lax.dot_general(a, b, (((0,), (0,)), ((), ())), preferred_element_type=jnp.float32)


def rows_of(i, tile):
    return pl.ds(pl.multiple_of(i * tile, tile), tile)


def pipelined(count, first_half, second_half, log_ref):
    @pl.when(count > 0)
    def _():
        log_ref[...] = first_half(0)

        def body(n, carry):
            ready = log_ref[...]
            following = first_half(n)
            second_half(n - 1, ready)
            log_ref[...] = following
            return carry

        lax.fori_loop(1, count, body, 0)
        second_half(count - 1, log_ref[...])


def own_kernel(
    meta, ids, src_ref, t_ref, w_ref, h_ref, acc_ref, keep_ref, send_ref, gw_ref, log_ref, task_ref, sem, *, parts
):
    row_blocks = ids.shape[1]
    tile = h_ref.shape[0] // row_blocks
    narrow = acc_ref.shape[1]
    b0 = meta[0] * 2

    def load(i):
        rows = rows_of(i, tile)
        return pltpu.make_async_copy(src_ref.at[rows, :], h_ref.at[rows, :], sem.at[i])

    def start_load(i, carry):
        load(i).start()
        return carry

    def wait_load(i, carry):
        load(i).wait()
        return carry

    lax.fori_loop(0, row_blocks, start_load, 0)
    acc_ref[...] = jnp.zeros_like(acc_ref)
    gw_ref[...] = jnp.zeros_like(gw_ref)

    def list_tasks(i, count):
        m0 = listed_flag(ids, i, b0)
        m1 = listed_flag(ids, i, b0 + 1)

        @pl.when(m0 + m1 > 0)
        def _():
            task_ref[0, count] = i
            task_ref[1, count] = m0
            task_ref[2, count] = m1

        return count + jnp.maximum(m0, m1)

    count = lax.fori_loop(0, row_blocks, list_tasks, jnp.int32(0))
    cols = pl.ds(pl.multiple_of(meta[0] * narrow, 128), narrow)

    def first_half(n):
        i = task_ref[0, n]
        past = -1 if isinstance(n, int) else task_ref[0, n - 1]
        lax.fori_loop(past + 1, i + 1, wait_load, 0)
        return nt(h_ref[rows_of(i, tile), :], w_ref[...])

    def second_half(n, logits):
        i = task_ref[0, n]
        rows = rows_of(i, tile)
        keep = jnp.where(lanes() < BLOCK, task_ref[1, n], task_ref[2, n]) > 0
        signal = signal_of(logits, t_ref[:, rows].T, b0 * BLOCK + lanes())
        g = jnp.where(keep, signal, 0.0).astype(jnp.bfloat16)
        acc_ref[rows, :] = jnp.dot(g, w_ref[:, cols], preferred_element_type=jnp.float32)
        gw_ref[...] += tn(g, h_ref[rows, :])

    pipelined(count, first_half, second_half, log_ref)
    done = jnp.where(count > 0, task_ref[0, jnp.maximum(count - 1, 0)], -1)
    lax.fori_loop(done + 1, row_blocks, wait_load, 0)
    core = meta[1]
    wide = keep_ref.shape[2]
    for y in range(parts // 2):
        mine = pl.ds(pl.multiple_of((2 * y + core) * wide, 128), wide)
        other = pl.ds(pl.multiple_of((2 * y + 1 - core) * wide, 128), wide)
        keep_ref[y] = gw_ref[:, mine]
        send_ref[y] = gw_ref[:, other].astype(jnp.bfloat16)


VM = pltpu.VMEM
SCALARS = [pl.BlockSpec(memory_space=pltpu.SMEM)] * 2


def in_vmem(n):
    return [pl.BlockSpec(memory_space=VM)] * n


def own_stage(meta, ids, hidden, targets, weight, narrow, parts):
    rows, d = hidden.shape
    owned = weight.shape[0]
    wide = d // parts
    row_blocks = ids.shape[1]
    return pl.pallas_call(
        functools.partial(own_kernel, parts=parts),
        in_specs=SCALARS + [pl.BlockSpec(memory_space=pl.ANY)] + in_vmem(2),
        out_specs=in_vmem(4),
        out_shape=[
            VM((rows, d), hidden.dtype),
            VM((rows, narrow), jnp.float32),
            jax.ShapeDtypeStruct((parts // 2, owned, wide), jnp.float32),
            jax.ShapeDtypeStruct((parts // 2, owned, wide), jnp.bfloat16),
        ],
        scratch_shapes=[
            VM((owned, d), jnp.float32),
            VM((rows // row_blocks, PAIR), jnp.float32),
            pltpu.SMEM((3, row_blocks), jnp.int32),
            pltpu.SemaphoreType.DMA((row_blocks,)),
        ],
        cost_estimate=pl.CostEstimate(flops=4 * rows * owned * d, bytes_accessed=1 << 22, transcendentals=0),
        compiler_params=pltpu.CompilerParams(vmem_limit_bytes=20 << 20),
        name="own_stage",
    )(meta, ids, hidden, targets, weight)


def far_kernel(meta, ids, h_ref, t_ref, acc_ref, *rest, shards, places):
    pieces = rest[: len(places)]
    *_, out_ref, w_ref, log_ref, task_ref, sem = rest[len(places) :]
    row_blocks = ids.shape[1]
    tile = h_ref.shape[0] // row_blocks
    narrow = acc_ref.shape[1]
    copies = [
        pltpu.make_async_copy(piece, w_ref.at[j, :, pl.ds(col, piece.shape[1])], sem.at[k])
        for k, (piece, (j, col)) in enumerate(zip(pieces, places))
    ]
    for copy in copies:
        copy.start()
    core = meta[1]
    names = []
    for s in shards:
        names += [meta[s] * 2 + core, meta[s] * 2 + 1 - core]

    def list_tasks(i, count):
        for j in range(0, len(names)):
            flag = listed_flag(ids, i, names[j])

            @pl.when(flag > 0)
            def _(j=j, count=count):
                fresh = count % 2
                task_ref[fresh, count // 2] = j
                task_ref[2 + fresh, count // 2] = names[j]
                task_ref[4, count // 2] = i
                task_ref[5, count // 2] = (1 + fresh) * BLOCK

            count = count + flag
        odd = count % 2

        @pl.when(odd > 0)
        def _():
            task_ref[1, count // 2] = 0
            task_ref[3, count // 2] = 0

        return count + odd

    count = lax.fori_loop(0, row_blocks, list_tasks, jnp.int32(0)) // 2
    cols = pl.ds(pl.multiple_of(meta[0] * narrow, 128), narrow)
    for copy in copies:
        copy.wait()

    def first_half(n):
        both = jnp.concatenate([w_ref[task_ref[0, n]], w_ref[task_ref[1, n]]], axis=0)
        return nt(h_ref[rows_of(task_ref[4, n], tile), :], both)

    def second_half(n, logits):
        rows = rows_of(task_ref[4, n], tile)
        lane = lanes()
        labels = jnp.where(lane < BLOCK, task_ref[2, n] * BLOCK + lane, (task_ref[3, n] - 1) * BLOCK + lane)
        signal = signal_of(logits, t_ref[:, rows].T, labels)
        g = jnp.where(lane < task_ref[5, n], signal, 0.0).astype(jnp.bfloat16)
        thin = jnp.concatenate([w_ref[task_ref[0, n], :, cols], w_ref[task_ref[1, n], :, cols]], axis=0)
        acc_ref[rows, :] += jnp.dot(g, thin, preferred_element_type=jnp.float32)

    pipelined(count, first_half, second_half, log_ref)
    if out_ref.dtype != jnp.float32:
        out_ref[...] = acc_ref[...].astype(out_ref.dtype)


def far_stage(meta, ids, hidden, targets, acc, pieces, places, shards, last):
    rows, d = hidden.shape
    narrow = acc.shape[1]
    row_blocks = ids.shape[1]
    blocks = 2 * len(shards)
    if last:
        shape = [jax.ShapeDtypeStruct((rows, narrow), jnp.bfloat16)]
    else:
        shape = [VM((rows, d), hidden.dtype), VM((rows, narrow), jnp.float32)]
    return pl.pallas_call(
        functools.partial(far_kernel, shards=shards, places=places),
        in_specs=SCALARS + in_vmem(3) + [pl.BlockSpec(memory_space=pl.ANY)] * len(pieces),
        out_specs=in_vmem(len(shape)),
        out_shape=shape,
        scratch_shapes=[
            VM((blocks, BLOCK, d), jnp.bfloat16),
            VM((rows // row_blocks, PAIR), jnp.float32),
            pltpu.SMEM((6, row_blocks * len(shards)), jnp.int32),
            pltpu.SemaphoreType.DMA((len(pieces),)),
        ],
        input_output_aliases={} if last else {2: 0, 4: 1},
        cost_estimate=pl.CostEstimate(flops=2 * rows * blocks * BLOCK * d, bytes_accessed=1 << 22, transcendentals=0),
        compiler_params=pltpu.CompilerParams(vmem_limit_bytes=20 << 20),
        name="far_stage",
    )(meta, ids, hidden, targets, acc, *pieces)


def merge_kernel(part, keep_ref, near_ref, mine_ref, *away_refs):
    row = part[0] // 2
    count = keep_ref.shape[0]
    mine_ref[...] = keep_ref[row] + near_ref[row].astype(jnp.float32)
    for k, away_ref in enumerate(away_refs):
        ahead = (row + k + 1) % count
        away_ref[...] = (keep_ref[ahead] + near_ref[ahead].astype(jnp.float32)).astype(away_ref.dtype)


def merge(part, keep, near):
    count, owned, wide = keep.shape
    outs = [jax.ShapeDtypeStruct((owned, wide), jnp.float32)]
    outs += [jax.ShapeDtypeStruct((owned, wide), jnp.bfloat16)] * (count - 1)
    return pl.pallas_call(
        merge_kernel,
        in_specs=SCALARS[:1] + in_vmem(2),
        out_specs=in_vmem(count),
        out_shape=outs,
        compiler_params=pltpu.CompilerParams(vmem_limit_bytes=8 << 20),
        name="merge",
    )(part.reshape(1), keep, near)


def finish_kernel(mine_ref, *refs):
    total = mine_ref[...]
    for got in refs[:-1]:
        total = total + got[...].astype(jnp.float32)
    refs[-1][...] = total.astype(refs[-1].dtype)


def finish(mine, got):
    return pl.pallas_call(
        finish_kernel,
        in_specs=in_vmem(1 + len(got)),
        out_specs=pl.BlockSpec(memory_space=VM),
        out_shape=jax.ShapeDtypeStruct(mine.shape, jnp.bfloat16),
        compiler_params=pltpu.CompilerParams(vmem_limit_bytes=8 << 20),
        name="finish",
    )(mine, *got)


def halves_kernel(a_ref, b_ref, low_ref, high_ref, sem):
    half = low_ref.shape[1]
    low = pltpu.make_async_copy(a_ref.at[:, :half], low_ref, sem.at[0])
    high = pltpu.make_async_copy(b_ref.at[:, half:], high_ref, sem.at[1])
    low.start()
    high.start()
    low.wait()
    high.wait()


def halves(a, b):
    whole = pl.BlockSpec(memory_space=pl.ANY)
    return pl.pallas_call(
        halves_kernel,
        in_specs=[whole] * 2,
        out_specs=[whole] * 2,
        out_shape=[jax.ShapeDtypeStruct((a.shape[0], a.shape[1] // 2), a.dtype)] * 2,
        scratch_shapes=[pltpu.SemaphoreType.DMA((2,))],
        compiler_params=pltpu.CompilerParams(vmem_limit_bytes=1 << 20),
        name="halves",
    )(a, b)


def local(hidden, weight, block_ids, targets):
    heads = lax.axis_size("head")
    parts = lax.axis_size("dp")
    head = lax.axis_index("head")
    part = lax.axis_index("dp")
    core = part % 2
    d = hidden.shape[1]
    narrow = d // heads
    half = heads // 2
    order = ring_order(heads)
    spot = np.argsort(order)
    table = np.zeros((heads, heads + 1), np.int32)
    for k in range(heads):
        table[k, 0] = k
        for step in range(1, half):
            table[k, 2 * step] = order[(spot[k] - step) % heads]
            table[k, 2 * step + 1] = order[(spot[k] + step) % heads]
        table[k, heads] = order[(spot[k] + half) % heads]
    column = np.arange(heads + 1) == 1
    meta = jnp.where(column, core, jnp.asarray(table)[head]).astype(jnp.int32)
    forward = [(order[k], order[(k + 1) % heads]) for k in range(heads)]
    backward = [(b, a) for a, b in forward]
    cores = [(p, p ^ 1) for p in range(parts)]
    ids = block_ids.T
    marks = pltpu.with_memory_space_constraint(targets.T, VM)

    own = lax.dynamic_slice_in_dim(weight, core * BLOCK, BLOCK, axis=0)
    fwd = lax.ppermute(own, "head", forward)
    bwd = lax.ppermute(own, "head", backward)

    rows, acc, keep, away = own_stage(meta, ids, hidden, marks, weight, narrow, parts)

    near = lax.ppermute(away, "dp", cores)
    mine, *away = merge(part, keep, near)
    got = [
        lax.ppermute(away[k - 1], "dp", [(p, (p + 2 * k) % parts) for p in range(parts)])
        for k in range(1, parts // 2)
    ]
    grad_weight = finish(mine, got)

    for step in range(1, half):
        fwd_swap = lax.ppermute(fwd, "dp", cores)
        bwd_swap = lax.ppermute(bwd, "dp", cores)
        pieces = [fwd, fwd_swap, bwd, bwd_swap]
        places = [(0, 0), (1, 0), (2, 0), (3, 0)]
        if step + 1 == half:
            fwd, bwd = halves(fwd, bwd)
        fwd = lax.ppermute(fwd, "head", forward)
        bwd = lax.ppermute(bwd, "head", backward)
        rows, acc = far_stage(
            meta, ids, rows, marks, acc, pieces, places, [2 * step, 2 * step + 1], False
        )

    fwd_swap = lax.ppermute(fwd, "dp", cores)
    bwd_swap = lax.ppermute(bwd, "dp", cores)
    pieces = [fwd, bwd, fwd_swap, bwd_swap]
    places = [(0, 0), (0, d // 2), (1, 0), (1, d // 2)]
    (grad_hidden,) = far_stage(meta, ids, rows, marks, acc, pieces, places, [heads], True)
    return (grad_hidden, grad_weight)


def solution(mesh):
    return jax.shard_map(
        local,
        mesh=mesh,
        in_specs=(P("dp", None), P("head", None), P("dp", None), P("dp", None)),
        out_specs=(P("dp", "head"), P("head", "dp")),
        check_vma=False,
    )
```

time: 423 us -> 145 us (0.34)
  the two profiles are of different devices: /device:TPU:0 before, /device:TPU:23 now
where the time goes in v1:
time: 145 us; the launch traced here: 144 us
  Pallas kernels  89 us (61%)
  waiting for transfers between devices  25.8 us (18%)
  starting transfers between devices  22.4 us (15%)
  local copies, waits for them, and re-layouts  5.78 us (4%)
    pallas_call x4, Pallas kernels, far_stage(): pl.pallas_call(functools.partial(far_kernel, shards=shards, places=places...  70.3 us
    pallas_call x1, Pallas kernels, own_stage(): pl.pallas_call(functools.partial(own_kernel, parts=parts), in_specs=SCALA...  17.5 us
    ppermute x1, waiting for transfers between devices, local(): lax.ppermute(away[k - 1], 'dp', [(p, (p + 2 * k) % parts) for p in range(...  11.9 us
    ppermute x3, waiting for transfers between devices, local(): bwd = lax.ppermute(bwd, 'head', backward)  10.8 us
    ppermute x1, starting transfers between devices, local(): near = lax.ppermute(away, 'dp', cores)  6.59 us
    unnamed x10, local copies, waits for them, and re-layouts  4.48 us
    ppermute x4, starting transfers between devices, local(): fwd_swap = lax.ppermute(fwd, 'dp', cores)  4.42 us
    ppermute x1, starting transfers between devices, local(): lax.ppermute(away[k - 1], 'dp', [(p, (p + 2 * k) % parts) for p in range(...  3.23 us
  transfers between devices with their start and end apart: 18, of which 5 were waited for; matrix products, arithmetic and copies ran while one was open for 0% of the time, Pallas kernels for 51%

profile of v1, /device:TPU:23, one launch (start us, length us, event | category | flops | bytes accessed | tf_op | source)
XLA Modules:
  0.0 144.4 jit_solution(10115651566503887655)
XLA Ops:
  0.6 1.3 constant_dynamic-slice_fusion
  1.9 0.2 collective-permute-start
  2.2 1.3 collective-permute-start.2
  3.5 0.7 select_bitcast_fusion.meta
  4.2 0.0 copy-start
  4.2 0.9 copy-done
  5.1 0.0 copy-start.1
  5.1 0.7 copy-done.1
  5.8 17.5 %own_stage.1 = (bf16[3072,4096]{1,0:T(8,128)(2,1)S(1)}, f32[3072,512]{1,0:T(8,128)S(1)}, f32[2,256,1024]{2,1,0:T(8,128)S(1)}, bf16[2,256,1024]{2,1,0:T(8,128)(2,1)S(1)}) custom-call(s32[9]{0:T(128)S(1)} %select_bitcast_fusion.meta, s32[8,12]{1,0:T(8,128)S(1)} %bitcast.10, bf16[3072,4096]{1,0:T(8,128)(2,1)} %src_ref.1, s32[8,3072]{1,0:T(8,128)S(1)} %bitcast.5, ...), custom_call_target="tpu_custom_call" | custom-call | flops 12884901888 | bytes 4194304 | tf_op jit(solution)/shard_map/own_stage/pallas_call | solution.py:151
  23.2 6.6 %collective-permute-start.16 = (bf16[2,256,1024]{2,1,0:T(8,128)(2,1)S(1)}, bf16[2,256,1024]{2,1,0:T(8,128)(2,1)S(1)}, u32[]{:S(2)}, u32[]{:S(2)}) collective-permute-start(bf16[2,256,1024]{2,1,0:T(8,128)(2,1)S(1)} %get-tuple-element.27), channel_id=1, source_target_pairs={{0,8},{8,0},{16,24},{24,16},{1,9},{9,1},{17,25},{25,17},{2,10},{10... | collective-permute-start | bytes 3145736 | tf_op jit(solution)/shard_map/ppermute | solution.py:358
  29.8 0.0 collective-permute-done.2.rest_2_
  29.8 0.0 collective-permute-start.6
  29.8 0.0 collective-permute-done.rest_0_
  29.8 1.5 %collective-permute-start.4 = (bf16[128,4096]{1,0:T(8,128)(2,1)S(1)}, bf16[128,4096]{1,0:T(8,128)(2,1)S(1)}, u32[]{:S(2)}, u32[]{:S(2)}) collective-permute-start(bf16[128,4096]{1,0:T(8,128)(2,1)S(1)} %collective-permute-done.rest_0_), channel_id=1, source_target_pairs={{0,2},{2,4},{4,6},{6,7},{7,5},{5,3},{3,1},{1,0},{8,10},{10,12},{12... | collective-permute-start | bytes 3145736 | tf_op jit(solution)/shard_map/ppermute | solution.py:373
  31.3 0.6 collective-permute-start.1
  31.9 0.0 collective-permute-start.3
  31.9 0.2 collective-permute-done.16.near_ref
  32.1 0.2 merge.1
  32.3 3.2 %collective-permute-start.17 = (bf16[256,1024]{1,0:T(8,128)(2,1)S(1)}, bf16[256,1024]{1,0:T(8,128)(2,1)S(1)}, u32[]{:S(2)}, u32[]{:S(2)}) collective-permute-start(bf16[256,1024]{1,0:T(8,128)(2,1)S(1)} %get-tuple-element.29), channel_id=1, source_target_pairs={{0,16},{8,24},{16,0},{24,8},{1,17},{9,25},{17,1},{25,9},{2,18},{10... | collective-permute-start | bytes 1572872 | tf_op jit(solution)/shard_map/ppermute | solution.py:361
  35.6 11.9 %collective-permute-done.17.refs_0_ = bf16[256,1024]{1,0:T(8,128)(2,1)S(1)} collective-permute-done((bf16[256,1024]{1,0:T(8,128)(2,1)S(1)}, bf16[256,1024]{1,0:T(8,128)(2,1)S(1)}, u32[]{:S(2)}, u32[]{:S(2)}) %collective-permute-start.17) | collective-permute-done | bytes 524320 | tf_op jit(solution)/shard_map/ppermute | solution.py:361
  47.5 0.9 finish.1
  48.4 6.1 %collective-permute-done.6.rest_2_ = bf16[128,4096]{1,0:T(8,128)(2,1)S(1)} collective-permute-done((bf16[128,4096]{1,0:T(8,128)(2,1)S(1)}, bf16[128,4096]{1,0:T(8,128)(2,1)S(1)}, u32[]{:S(2)}, u32[]{:S(2)}) %collective-permute-start.6) | collective-permute-done | bytes 1048608 | tf_op jit(solution)/shard_map/ppermute | solution.py:374
  54.5 0.9 collective-permute-start.7
  55.4 0.0 collective-permute-start.10
  55.4 0.0 collective-permute-done.4.rest_0_
  55.4 0.3 collective-permute-start.5
  55.7 0.0 collective-permute-done.1.rest_1_
  55.7 1.5 %collective-permute-start.8 = (bf16[128,4096]{1,0:T(8,128)(2,1)S(1)}, bf16[128,4096]{1,0:T(8,128)(2,1)S(1)}, u32[]{:S(2)}, u32[]{:S(2)}) collective-permute-start(bf16[128,4096]{1,0:T(8,128)(2,1)S(1)} %collective-permute-done.4.rest_0_), channel_id=1, source_target_pairs={{0,2},{2,4},{4,6},{6,7},{7,5},{5,3},{3,1},{1,0},{8,10},{10,12},{12... | collective-permute-start | bytes 3145736 | tf_op jit(solution)/shard_map/ppermute | solution.py:373
  57.1 0.0 collective-permute-done.3.rest_3_
  57.1 0.0 copy-start.3
  57.2 1.0 copy-done.3
  58.1 17.2 %far_stage.4 = (bf16[3072,4096]{1,0:T(8,128)(2,1)S(1)}, f32[3072,512]{1,0:T(8,128)S(1)}) custom-call(s32[9]{0:T(128)S(1)} %select_bitcast_fusion.meta, s32[8,12]{1,0:T(8,128)S(1)} %bitcast.11, bf16[3072,4096]{1,0:T(8,128)(2,1)S(1)} %get-tuple-element.16.h_ref, s32[8,3072]{1,0:T(8,128)S(1)} %bitcast.6, ...), custom_call_target="tpu_custom_call", output_to_operand_aliasing={{0}: (2, {}), {1}: (4, {})} | custom-call | flops 12884901888 | bytes 4194304 | tf_op jit(solution)/shard_map/far_stage/pallas_call | solution.py:244
  75.4 4.7 %collective-permute-done.10.rest_2_.b_ref = bf16[128,4096]{1,0:T(8,128)(2,1)S(1)} collective-permute-done((bf16[128,4096]{1,0:T(8,128)(2,1)S(1)}, bf16[128,4096]{1,0:T(8,128)(2,1)S(1)}, u32[]{:S(2)}, u32[]{:S(2)}) %collective-permute-start.10) | collective-permute-done | bytes 1048608 | tf_op jit(solution)/shard_map/ppermute | solution.py:374
  80.1 2.9 %collective-permute-done.8.rest_0_.a_ref = bf16[128,4096]{1,0:T(8,128)(2,1)S(1)} collective-permute-done((bf16[128,4096]{1,0:T(8,128)(2,1)S(1)}, bf16[128,4096]{1,0:T(8,128)(2,1)S(1)}, u32[]{:S(2)}, u32[]{:S(2)}) %collective-permute-start.8) | collective-permute-done | bytes 1048608 | tf_op jit(solution)/shard_map/ppermute | solution.py:373
  83.0 0.1 halves.1
  83.1 0.1 collective-permute-start.12
  83.1 1.6 %collective-permute-start.13 = (bf16[128,2048]{1,0:T(8,128)(2,1)S(1)}, bf16[128,2048]{1,0:T(8,128)(2,1)S(1)}, u32[]{:S(2)}, u32[]{:S(2)}) collective-permute-start(bf16[128,2048]{1,0:T(8,128)(2,1)S(1)} %get-tuple-element.25), channel_id=1, source_target_pairs={{2,0},{4,2},{6,4},{7,6},{5,7},{3,5},{1,3},{0,1},{10,8},{12,10},{14... | collective-permute-start | bytes 1572872 | tf_op jit(solution)/shard_map/ppermute | solution.py:374
  84.7 1.1 collective-permute-start.11
  85.8 0.0 collective-permute-done.5.rest_1_
  85.8 0.0 collective-permute-start.9
  85.8 0.0 collective-permute-done.7.rest_3_
  85.8 0.0 copy-start.2
  85.8 1.0 copy-done.2
  86.8 14.3 %far_stage.5 = (bf16[3072,4096]{1,0:T(8,128)(2,1)S(1)}, f32[3072,512]{1,0:T(8,128)S(1)}) custom-call(s32[9]{0:T(128)S(1)} %select_bitcast_fusion.meta, s32[8,12]{1,0:T(8,128)S(1)} %bitcast.12, bf16[3072,4096]{1,0:T(8,128)(2,1)S(1)} %get-tuple-element.18.h_ref, s32[8,3072]{1,0:T(8,128)S(1)} %bitcast.7, ...), custom_call_target="tpu_custom_call", output_to_operand_aliasing={{0}: (2, {}), {1}: (4, {})} | custom-call | flops 12884901888 | bytes 4194304 | tf_op jit(solution)/shard_map/far_stage/pallas_call | solution.py:244
  101.1 0.0 collective-permute-done.12.rest_0_
  101.1 3.5 %collective-permute-start.14 = (bf16[128,2048]{1,0:T(8,128)(2,1)S(1)}, bf16[128,2048]{1,0:T(8,128)(2,1)S(1)}, u32[]{:S(2)}, u32[]{:S(2)}) collective-permute-start(bf16[128,2048]{1,0:T(8,128)(2,1)S(1)} %collective-permute-done.12.rest_0_), channel_id=1, source_target_pairs={{0,8},{8,0},{16,24},{24,16},{1,9},{9,1},{17,25},{25,17},{2,10},{10... | collective-permute-start | bytes 1572872 | tf_op jit(solution)/shard_map/ppermute | solution.py:379
  104.6 0.0 collective-permute-done.13.rest_1_
  104.6 0.1 collective-permute-start.15
  104.7 0.0 collective-permute-done.11.rest_3_
  104.7 0.0 copy-start.4
  104.7 0.0 collective-permute-done.9.rest_1_
  104.7 1.0 copy-done.4
  105.7 23.1 %far_stage.6 = (bf16[3072,4096]{1,0:T(8,128)(2,1)S(1)}, f32[3072,512]{1,0:T(8,128)S(1)}) custom-call(s32[9]{0:T(128)S(1)} %select_bitcast_fusion.meta, s32[8,12]{1,0:T(8,128)S(1)} %bitcast.13, bf16[3072,4096]{1,0:T(8,128)(2,1)S(1)} %get-tuple-element.20.h_ref, s32[8,3072]{1,0:T(8,128)S(1)} %bitcast.8, ...), custom_call_target="tpu_custom_call", output_to_operand_aliasing={{0}: (2, {}), {1}: (4, {})} | custom-call | flops 12884901888 | bytes 4194304 | tf_op jit(solution)/shard_map/far_stage/pallas_call | solution.py:244
  128.8 0.0 collective-permute-done.14.rest_2_
  128.8 0.0 collective-permute-done.15.rest_3_
  128.8 15.6 %far_stage.7 = bf16[3072,512]{1,0:T(8,128)(2,1)} custom-call(s32[9]{0:T(128)S(1)} %select_bitcast_fusion.meta, s32[8,12]{1,0:T(8,128)S(1)} %bitcast.14, bf16[3072,4096]{1,0:T(8,128)(2,1)S(1)} %get-tuple-element.22.h_ref, s32[8,3072]{1,0:T(8,128)S(1)} %bitcast.9, f32[3072,512]{1,0:T(8,128)S(1)} %get-tuple-element.23.acc_ref, ...), custom_call_target="tpu_custom_call" | custom-call | flops 6442450944 | bytes 4194304 | tf_op jit(solution)/shard_map/far_stage/pallas_call | solution.py:244
Async XLA Ops:
  1.9 27.9 %collective-permute-start = (bf16[128,4096]{1,0:T(8,128)(2,1)S(1)}, bf16[128,4096]{1,0:T(8,128)(2,1)S(1)}, u32[]{:S(2)}, u32[]{:S(2)}) collective-permute-start(bf16[128,4096]{1,0:T(8,128)(2,1)S(1)} %constant_dynamic-slice_fusion), channel_id=1, source_target_pairs={{0,2},{2,4},{4,6},{6,7},{7,5},{5,3},{3,1},{1,0},{8,10},{10,12},{12... | collective-permute-start | bytes 3145736 | tf_op jit(solution)/shard_map/ppermute | solution.py:353
  2.2 27.6 %collective-permute-start.2 = (bf16[128,4096]{1,0:T(8,128)(2,1)S(1)}, bf16[128,4096]{1,0:T(8,128)(2,1)S(1)}, u32[]{:S(2)}, u32[]{:S(2)}) collective-permute-start(bf16[128,4096]{1,0:T(8,128)(2,1)S(1)} %constant_dynamic-slice_fusion), channel_id=1, source_target_pairs={{2,0},{4,2},{6,4},{7,6},{5,7},{3,5},{1,3},{0,1},{10,8},{12,10},{14... | collective-permute-start | bytes 3145736 | tf_op jit(solution)/shard_map/ppermute | solution.py:354
  4.2 0.9 copy-start
  5.1 0.7 copy-start.1
  23.2 8.9 %collective-permute-start.16 = (bf16[2,256,1024]{2,1,0:T(8,128)(2,1)S(1)}, bf16[2,256,1024]{2,1,0:T(8,128)(2,1)S(1)}, u32[]{:S(2)}, u32[]{:S(2)}) collective-permute-start(bf16[2,256,1024]{2,1,0:T(8,128)(2,1)S(1)} %get-tuple-element.27), channel_id=1, source_target_pairs={{0,8},{8,0},{16,24},{24,16},{1,9},{9,1},{17,25},{25,17},{2,10},{10... | collective-permute-start | bytes 3145736 | tf_op jit(solution)/shard_map/ppermute | solution.py:358
  29.8 24.6 %collective-permute-start.6 = (bf16[128,4096]{1,0:T(8,128)(2,1)S(1)}, bf16[128,4096]{1,0:T(8,128)(2,1)S(1)}, u32[]{:S(2)}, u32[]{:S(2)}) collective-permute-start(bf16[128,4096]{1,0:T(8,128)(2,1)S(1)} %collective-permute-done.2.rest_2_), channel_id=1, source_target_pairs={{2,0},{4,2},{6,4},{7,6},{5,7},{3,5},{1,3},{0,1},{10,8},{12,10},{14... | collective-permute-start | bytes 3145736 | tf_op jit(solution)/shard_map/ppermute | solution.py:374
  29.8 25.6 %collective-permute-start.4 = (bf16[128,4096]{1,0:T(8,128)(2,1)S(1)}, bf16[128,4096]{1,0:T(8,128)(2,1)S(1)}, u32[]{:S(2)}, u32[]{:S(2)}) collective-permute-start(bf16[128,4096]{1,0:T(8,128)(2,1)S(1)} %collective-permute-done.rest_0_), channel_id=1, source_target_pairs={{0,2},{2,4},{4,6},{6,7},{7,5},{5,3},{3,1},{1,0},{8,10},{10,12},{12... | collective-permute-start | bytes 3145736 | tf_op jit(solution)/shard_map/ppermute | solution.py:373
  31.3 24.4 %collective-permute-start.1 = (bf16[128,4096]{1,0:T(8,128)(2,1)S(1)}, bf16[128,4096]{1,0:T(8,128)(2,1)S(1)}, u32[]{:S(2)}, u32[]{:S(2)}) collective-permute-start(bf16[128,4096]{1,0:T(8,128)(2,1)S(1)} %collective-permute-done.rest_0_), channel_id=1, source_target_pairs={{0,8},{8,0},{16,24},{24,16},{1,9},{9,1},{17,25},{25,17},{2,10},{10... | collective-permute-start | bytes 3145736 | tf_op jit(solution)/shard_map/ppermute | solution.py:367
  31.9 25.2 %collective-permute-start.3 = (bf16[128,4096]{1,0:T(8,128)(2,1)S(1)}, bf16[128,4096]{1,0:T(8,128)(2,1)S(1)}, u32[]{:S(2)}, u32[]{:S(2)}) collective-permute-start(bf16[128,4096]{1,0:T(8,128)(2,1)S(1)} %collective-permute-done.2.rest_2_), channel_id=1, source_target_pairs={{0,8},{8,0},{16,24},{24,16},{1,9},{9,1},{17,25},{25,17},{2,10},{10... | collective-permute-start | bytes 3145736 | tf_op jit(solution)/shard_map/ppermute | solution.py:368
  32.3 15.1 %collective-permute-start.17 = (bf16[256,1024]{1,0:T(8,128)(2,1)S(1)}, bf16[256,1024]{1,0:T(8,128)(2,1)S(1)}, u32[]{:S(2)}, u32[]{:S(2)}) collective-permute-start(bf16[256,1024]{1,0:T(8,128)(2,1)S(1)} %get-tuple-element.29), channel_id=1, source_target_pairs={{0,16},{8,24},{16,0},{24,8},{1,17},{9,25},{17,1},{25,9},{2,18},{10... | collective-permute-start | bytes 1572872 | tf_op jit(solution)/shard_map/ppermute | solution.py:361
  54.5 31.3 %collective-permute-start.7 = (bf16[128,4096]{1,0:T(8,128)(2,1)S(1)}, bf16[128,4096]{1,0:T(8,128)(2,1)S(1)}, u32[]{:S(2)}, u32[]{:S(2)}) collective-permute-start(bf16[128,4096]{1,0:T(8,128)(2,1)S(1)} %collective-permute-done.6.rest_2_), channel_id=1, source_target_pairs={{0,8},{8,0},{16,24},{24,16},{1,9},{9,1},{17,25},{25,17},{2,10},{10... | collective-permute-start | bytes 3145736 | tf_op jit(solution)/shard_map/ppermute | solution.py:368
  55.4 24.7 %collective-permute-start.10 = (bf16[128,4096]{1,0:T(8,128)(2,1)S(1)}, bf16[128,4096]{1,0:T(8,128)(2,1)S(1)}, u32[]{:S(2)}, u32[]{:S(2)}) collective-permute-start(bf16[128,4096]{1,0:T(8,128)(2,1)S(1)} %collective-permute-done.6.rest_2_), channel_id=1, source_target_pairs={{2,0},{4,2},{6,4},{7,6},{5,7},{3,5},{1,3},{0,1},{10,8},{12,10},{14... | collective-permute-start | bytes 3145736 | tf_op jit(solution)/shard_map/ppermute | solution.py:374
  55.4 30.4 %collective-permute-start.5 = (bf16[128,4096]{1,0:T(8,128)(2,1)S(1)}, bf16[128,4096]{1,0:T(8,128)(2,1)S(1)}, u32[]{:S(2)}, u32[]{:S(2)}) collective-permute-start(bf16[128,4096]{1,0:T(8,128)(2,1)S(1)} %collective-permute-done.4.rest_0_), channel_id=1, source_target_pairs={{0,8},{8,0},{16,24},{24,16},{1,9},{9,1},{17,25},{25,17},{2,10},{10... | collective-permute-start | bytes 3145736 | tf_op jit(solution)/shard_map/ppermute | solution.py:367
  55.7 27.3 %collective-permute-start.8 = (bf16[128,4096]{1,0:T(8,128)(2,1)S(1)}, bf16[128,4096]{1,0:T(8,128)(2,1)S(1)}, u32[]{:S(2)}, u32[]{:S(2)}) collective-permute-start(bf16[128,4096]{1,0:T(8,128)(2,1)S(1)} %collective-permute-done.4.rest_0_), channel_id=1, source_target_pairs={{0,2},{2,4},{4,6},{6,7},{7,5},{5,3},{3,1},{1,0},{8,10},{10,12},{12... | collective-permute-start | bytes 3145736 | tf_op jit(solution)/shard_map/ppermute | solution.py:373
  57.1 1.0 copy-start.3
  83.1 18.0 %collective-permute-start.12 = (bf16[128,2048]{1,0:T(8,128)(2,1)S(1)}, bf16[128,2048]{1,0:T(8,128)(2,1)S(1)}, u32[]{:S(2)}, u32[]{:S(2)}) collective-permute-start(bf16[128,2048]{1,0:T(8,128)(2,1)S(1)} %get-tuple-element.24), channel_id=1, source_target_pairs={{0,2},{2,4},{4,6},{6,7},{7,5},{5,3},{3,1},{1,0},{8,10},{10,12},{12... | collective-permute-start | bytes 1572872 | tf_op jit(solution)/shard_map/ppermute | solution.py:373
  83.1 21.5 %collective-permute-start.13 = (bf16[128,2048]{1,0:T(8,128)(2,1)S(1)}, bf16[128,2048]{1,0:T(8,128)(2,1)S(1)}, u32[]{:S(2)}, u32[]{:S(2)}) collective-permute-start(bf16[128,2048]{1,0:T(8,128)(2,1)S(1)} %get-tuple-element.25), channel_id=1, source_target_pairs={{2,0},{4,2},{6,4},{7,6},{5,7},{3,5},{1,3},{0,1},{10,8},{12,10},{14... | collective-permute-start | bytes 1572872 | tf_op jit(solution)/shard_map/ppermute | solution.py:374
  84.7 20.0 %collective-permute-start.11 = (bf16[128,4096]{1,0:T(8,128)(2,1)S(1)}, bf16[128,4096]{1,0:T(8,128)(2,1)S(1)}, u32[]{:S(2)}, u32[]{:S(2)}) collective-permute-start(bf16[128,4096]{1,0:T(8,128)(2,1)S(1)} %collective-permute-done.10.rest_2_.b_ref), channel_id=1, source_target_pairs={{0,8},{8,0},{16,24},{24,16},{1,9},{9,1},{17,25},{25,17},{2,10},{10... | collective-permute-start | bytes 3145736 | tf_op jit(solution)/shard_map/ppermute | solution.py:368
  85.8 18.9 %collective-permute-start.9 = (bf16[128,4096]{1,0:T(8,128)(2,1)S(1)}, bf16[128,4096]{1,0:T(8,128)(2,1)S(1)}, u32[]{:S(2)}, u32[]{:S(2)}) collective-permute-start(bf16[128,4096]{1,0:T(8,128)(2,1)S(1)} %collective-permute-done.8.rest_0_.a_ref), channel_id=1, source_target_pairs={{0,8},{8,0},{16,24},{24,16},{1,9},{9,1},{17,25},{25,17},{2,10},{10... | collective-permute-start | bytes 3145736 | tf_op jit(solution)/shard_map/ppermute | solution.py:367
  85.8 1.0 copy-start.2
  101.1 27.7 %collective-permute-start.14 = (bf16[128,2048]{1,0:T(8,128)(2,1)S(1)}, bf16[128,2048]{1,0:T(8,128)(2,1)S(1)}, u32[]{:S(2)}, u32[]{:S(2)}) collective-permute-start(bf16[128,2048]{1,0:T(8,128)(2,1)S(1)} %collective-permute-done.12.rest_0_), channel_id=1, source_target_pairs={{0,8},{8,0},{16,24},{24,16},{1,9},{9,1},{17,25},{25,17},{2,10},{10... | collective-permute-start | bytes 1572872 | tf_op jit(solution)/shard_map/ppermute | solution.py:379
  104.6 24.2 %collective-permute-start.15 = (bf16[128,2048]{1,0:T(8,128)(2,1)S(1)}, bf16[128,2048]{1,0:T(8,128)(2,1)S(1)}, u32[]{:S(2)}, u32[]{:S(2)}) collective-permute-start(bf16[128,2048]{1,0:T(8,128)(2,1)S(1)} %collective-permute-done.13.rest_1_), channel_id=1, source_target_pairs={{0,8},{8,0},{16,24},{24,16},{1,9},{9,1},{17,25},{25,17},{2,10},{10... | collective-permute-start | bytes 1572872 | tf_op jit(solution)/shard_map/ppermute | solution.py:380
  104.7 1.0 copy-start.4
